TPU v7x, 32 devices: a whole 2x2x4 slice. The times are simulated.
32 devices in a mesh: dp: 2 (over x), seq: 16 (over z, y, core).
Axes of the slice: x: 2, y: 2, z: 4, core: 2. Of those that a mesh axis runs over, the one named last changes fastest.
Arguments:
- pixels: bfloat16 [4096, 768], P(('dp', 'seq')), may hold values from -6 to 6
- mask: int32 [4096], P(('dp', 'seq')), may hold values 0 or 1
- image_count: int32 [2, 6], P('dp'), may hold values from 1 to 1024, 2048 in all within a row
- image_width: int32 [2, 6], P('dp'), may hold values from 4 to 63
- gsd_index: int32 [2, 6], P('dp'), may hold values from 0 to 8
- step: int32 [1], replicated, may hold values from 2 to 20
- master: float32 [17551360], P(('dp', 'seq')), as said below
- moment_one: float32 [17551360], P(('dp', 'seq')), as said below
- moment_two: float32 [17551360], P(('dp', 'seq')), as said below
Outputs:
- new_master: float32 [17551360], P(('dp', 'seq'))
- new_moment_one: float32 [17551360], P(('dp', 'seq'))
- new_moment_two: float32 [17551360], P(('dp', 'seq'))
- loss: float32 [1], replicated
- grad_norm: float32 [1], replicated
Inputs may be any that keep to these rules, and one draw needn't show every extreme that they name: master holds each weight drawn by its fan-in, gains near 1. moment_two is positive. moment_one takes both signs.
All inputs are finite; a program needn't handle non-finite values. No bound on the sum of `mask` on one device may be relied on, other than what follows from the above.
Results may differ from a plain program's by a relative error of at most 0.0024.
The roundings to bfloat16 on the way count: a program that leaves them out, or rounds other values in their place, can miss the bound.
Values may be sent and summed in bfloat16 or wider, within the bound.
A program may use at most 512 MiB of HBM per device.

v0:
```python
import math
import jax
import jax.numpy as jnp
from jax import lax
from jax.sharding import PartitionSpec as P

D = 1024
HEADS = 16
FF = 4096
DD = 512
DHEADS = 16
DFF = 2048
PATCH = 16
PIX = 768
LOWPIX = 192
clip_level = 0.0001
peak_rate = 0.1
warm_steps = 10.0
decay_rate = 0.05
adam_eps = 1e-12


def param_shapes():
    return [
        (PIX, D),
        (D,),
        (4, D),
        (D, 3 * D),
        (D, D),
        (D,),
        (D, FF),
        (FF,),
        (FF, D),
        (D,),
        (D, DD),
        (DD,),
        (DD,),
        (4, DD),
        (DD, 3 * DD),
        (DD, DD),
        (DD,),
        (DD, DFF),
        (DFF,),
        (DFF, DD),
        (DD,),
        (DD, PIX),
        (PIX,),
        (DD, LOWPIX),
        (LOWPIX,),
    ]


def unpack(flat):
    pieces = []
    offset = 0
    for shape in param_shapes():
        length = math.prod(shape)
        pieces.append(lax.slice_in_dim(flat, offset, offset + length).reshape(shape))
        offset += length
    return pieces


def matmul(a, b):
    return jnp.dot(a, b, preferred_element_type=jnp.float32)


def outer(a, b):
    return lax.dot_general(a, b, (((0,), (0,)), ((), ())), preferred_element_type=jnp.float32)


def back_mul(a, weight):
    return lax.dot_general(a, weight, (((1,), (1,)), ((), ())), preferred_element_type=jnp.float32)


def layer_norm(x, gain, shift):
    centred = x - jnp.mean(x, axis=-1, keepdims=True)
    return (
        centred * lax.rsqrt(jnp.mean(centred * centred, axis=-1, keepdims=True) + 1e-06) * gain
        + shift
    )


def geometry(counts, widths, ground, places):
    ends = jnp.cumsum(counts)
    starts = ends - counts
    inside = ((places[:, None] >= starts[None, :]) & (places[:, None] < ends[None, :])).astype(
        jnp.int32
    )
    image = jnp.sum(inside * jnp.arange(counts.shape[0], dtype=jnp.int32)[None, :], axis=1)
    start = jnp.sum(inside * starts[None, :], axis=1)
    width = jnp.sum(inside * widths[None, :], axis=1)
    level = jnp.sum(inside * ground[None, :], axis=1)
    local = places - start
    row_num = local // width
    col_num = local - row_num * width
    ratio = jnp.exp2(level.astype(jnp.float32) * 0.25)
    return (image, local, row_num.astype(jnp.float32) * ratio, col_num.astype(jnp.float32) * ratio)


def position_code(row_pos, col_pos, width):
    quarter = width // 4
    freqs = jnp.power(10000.0, -jnp.arange(quarter, dtype=jnp.float32) / quarter)
    row_ang = row_pos[:, None] * freqs[None, :]
    col_ang = col_pos[:, None] * freqs[None, :]
    return jnp.concatenate(
        [jnp.sin(row_ang), jnp.cos(row_ang), jnp.sin(col_ang), jnp.cos(col_ang)], axis=1
    )


def pool_table():
    values = 3 * PATCH * PATCH
    index = jnp.arange(values, dtype=jnp.int32)
    channel = index % 3
    cell = index // 3
    row_num = cell // PATCH
    col_num = cell % PATCH
    target = (row_num // 2 * (PATCH // 2) + col_num // 2) * 3 + channel
    return (target[:, None] == jnp.arange(values // 4, dtype=jnp.int32)[None, :]).astype(
        jnp.float32
    ) * 0.25


def masked_scores(queries, keys, query_image, key_image, key_seen, scale):
    raw = jnp.einsum("rhd,khd->hrk", queries, keys, preferred_element_type=jnp.float32) * scale
    allowed = (query_image[:, None] == key_image[None, :]) & (key_seen[None, :] > 0)
    return jnp.where(allowed[None], raw, -1e30)


def attend(queries, keys, values, key_seen, query_image, key_image, scale):
    scores = masked_scores(queries, keys, query_image, key_image, key_seen, scale)
    top = jnp.max(scores, axis=-1)
    mass = jnp.sum(jnp.where(scores > -1e29, jnp.exp(scores - top[..., None]), 0.0), axis=-1)
    lse = top + jnp.log(mass)
    probs = jnp.exp(scores - lse[..., None]).astype(jnp.bfloat16)
    out = jnp.einsum("hrk,khd->rhd", probs, values, preferred_element_type=jnp.float32)
    return (out, lse)


def attend_back(queries, keys, values, key_seen, query_image, key_image, out, lse, grad_out, scale):
    rows, heads, depth = queries.shape
    dterm = jnp.transpose(jnp.sum(grad_out.astype(jnp.float32) * out, axis=-1))
    scores = masked_scores(queries, keys, query_image, key_image, key_seen, scale)
    probs = jnp.exp(scores - lse[..., None])
    dprob = jnp.einsum("rhd,khd->hrk", grad_out, values, preferred_element_type=jnp.float32)
    dscore = (probs * (dprob - dterm[..., None])).astype(jnp.bfloat16)
    probs_low = probs.astype(jnp.bfloat16)
    grad_queries = jnp.einsum("hrk,khd->rhd", dscore, keys, preferred_element_type=jnp.float32)
    count = rows * lax.axis_size("seq")
    grad_keys = (
        jnp.einsum("hrk,rhd->khd", dscore, queries, preferred_element_type=jnp.float32) * scale
    )
    grad_values = jnp.einsum(
        "hrk,rhd->khd", probs_low, grad_out, preferred_element_type=jnp.float32
    )
    grad_kv = lax.psum_scatter(
        jnp.concatenate([grad_keys.reshape(count, -1), grad_values.reshape(count, -1)], axis=1),
        "seq",
        scatter_dimension=0,
        tiled=True,
    )
    return (grad_queries * scale, grad_kv)


def block_forward(x, weights, seen, query_image, key_image, heads):
    norms, qkv_w, out_w, out_b, up_w, up_b, down_w, down_b = weights
    gains = norms.astype(jnp.float32)
    rows, width = x.shape
    depth = width // heads
    scale = depth ** (-0.5)
    normed = layer_norm(x, gains[0], gains[1]).astype(jnp.bfloat16)
    mixed = matmul(normed, qkv_w).astype(jnp.bfloat16)
    queries = mixed[:, :width].reshape(rows, heads, depth)
    all_keys, all_values, all_seen = (
        lax.all_gather(mixed[:, width : 2 * width], "seq", axis=0, tiled=True),
        lax.all_gather(mixed[:, 2 * width :], "seq", axis=0, tiled=True),
        lax.all_gather(seen, "seq", axis=0, tiled=True),
    )
    all_keys = all_keys.reshape(-1, heads, depth)
    all_values = all_values.reshape(-1, heads, depth)
    out, lse = attend(queries, all_keys, all_values, all_seen, query_image, key_image, scale)
    attended = out.reshape(rows, width).astype(jnp.bfloat16)
    resid = x + matmul(attended, out_w) + out_b.astype(jnp.float32)
    normed_two = layer_norm(resid, gains[2], gains[3]).astype(jnp.bfloat16)
    pre = matmul(normed_two, up_w) + up_b.astype(jnp.float32)
    hidden_act = jax.nn.gelu(pre, approximate=False).astype(jnp.bfloat16)
    result = resid + matmul(hidden_act, down_w) + down_b.astype(jnp.float32)
    kept = (
        x,
        normed,
        queries,
        all_keys,
        all_values,
        all_seen,
        out,
        lse,
        attended,
        resid,
        normed_two,
        pre,
        hidden_act,
    )
    return (result, kept)


def block_backward(grad, weights, kept, query_image, key_image, heads):
    norms, qkv_w, out_w, out_b, up_w, up_b, down_w, down_b = weights
    gains = norms.astype(jnp.float32)
    (
        x,
        normed,
        queries,
        all_keys,
        all_values,
        all_seen,
        out,
        lse,
        attended,
        resid,
        normed_two,
        pre,
        hidden_act,
    ) = kept
    rows, width = x.shape
    depth = width // heads
    grad_low = grad.astype(jnp.bfloat16)
    grad_down = outer(hidden_act, grad_low)
    grad_down_b = jnp.sum(grad, axis=0)
    _, gelu_back = jax.vjp(lambda value: jax.nn.gelu(value, approximate=False), pre)
    (grad_pre,) = gelu_back(back_mul(grad_low, down_w))
    pre_low = grad_pre.astype(jnp.bfloat16)
    grad_up = outer(normed_two, pre_low)
    grad_up_b = jnp.sum(grad_pre, axis=0)
    _, norm_two_back = jax.vjp(layer_norm, resid, gains[2], gains[3])
    grad_resid, grad_gain_two, grad_shift_two = norm_two_back(back_mul(pre_low, up_w))
    grad_resid = grad_resid + grad
    resid_low = grad_resid.astype(jnp.bfloat16)
    grad_out = outer(attended, resid_low)
    grad_out_b = jnp.sum(grad_resid, axis=0)
    grad_attended = back_mul(resid_low, out_w).astype(jnp.bfloat16).reshape(rows, heads, depth)
    grad_queries, grad_kv = attend_back(
        queries,
        all_keys,
        all_values,
        all_seen,
        query_image,
        key_image,
        out,
        lse,
        grad_attended,
        depth ** (-0.5),
    )
    mixed_low = jnp.concatenate([grad_queries.reshape(rows, width), grad_kv], axis=1).astype(
        jnp.bfloat16
    )
    grad_qkv = outer(normed, mixed_low)
    _, norm_one_back = jax.vjp(layer_norm, x, gains[0], gains[1])
    grad_x, grad_gain_one, grad_shift_one = norm_one_back(back_mul(mixed_low, qkv_w))
    grad_norms = jnp.stack([grad_gain_one, grad_shift_one, grad_gain_two, grad_shift_two])
    return (
        grad_x + grad_resid,
        [grad_norms, grad_qkv, grad_out, grad_out_b, grad_up, grad_up_b, grad_down, grad_down_b],
    )


def body(pixels, mask, image_count, image_width, gsd_index, step, master, moment_one, moment_two):
    flat = lax.all_gather(master.astype(jnp.bfloat16), ("dp", "seq"), axis=0, tiled=True)
    weights = unpack(flat)
    rows = pixels.shape[0]
    group_rows = rows * lax.axis_size("seq")
    places = lax.axis_index("seq") * rows + jnp.arange(rows, dtype=jnp.int32)
    counts, widths, ground = (image_count[0], image_width[0], gsd_index[0])
    query_image, local, row_pos, col_pos = geometry(counts, widths, ground, places)
    key_image = geometry(counts, widths, ground, jnp.arange(group_rows, dtype=jnp.int32))[0]
    hidden = ((mask == 1) & (local != 0)).astype(jnp.float32)
    count_local = jnp.sum(hidden)
    count = lax.psum(count_local, ("dp", "seq"))
    embedded = (
        matmul(pixels, weights[0])
        + weights[1].astype(jnp.float32)
        + position_code(row_pos, col_pos, D)
    )
    encoded, enc_kept = block_forward(
        embedded, weights[2:10], (1.0 - hidden).astype(jnp.bfloat16), query_image, key_image, HEADS
    )
    encoded_low = encoded.astype(jnp.bfloat16)
    projected = matmul(encoded_low, weights[10]) + weights[11].astype(jnp.float32)
    dec_in = jnp.where(
        hidden[:, None] > 0, weights[12].astype(jnp.float32)[None, :], projected
    ) + position_code(row_pos, col_pos, DD)
    decoded, dec_kept = block_forward(
        dec_in, weights[13:21], jnp.ones((rows,), jnp.bfloat16), query_image, key_image, DHEADS
    )
    decoded_low = decoded.astype(jnp.bfloat16)
    high = matmul(decoded_low, weights[21]) + weights[22].astype(jnp.float32)
    low_pred = matmul(decoded_low, weights[23]) + weights[24].astype(jnp.float32)
    table = pool_table()
    pix_wide = pixels.astype(jnp.float32)
    low_target = jnp.dot(
        pix_wide, table, precision=lax.Precision.HIGHEST, preferred_element_type=jnp.float32
    )
    high_target = pix_wide - jnp.dot(
        low_target,
        4.0 * table.T,
        precision=lax.Precision.HIGHEST,
        preferred_element_type=jnp.float32,
    )
    per_patch = jnp.mean(jnp.abs(high - high_target), axis=-1) + jnp.mean(
        (low_pred - low_target) ** 2, axis=-1
    )
    loss_local = jnp.sum(hidden * per_patch)
    grad_high = hidden[:, None] * jnp.sign(high - high_target) / PIX
    grad_low_pred = hidden[:, None] * 2.0 * (low_pred - low_target) / LOWPIX
    high_low = grad_high.astype(jnp.bfloat16)
    lowband_low = grad_low_pred.astype(jnp.bfloat16)
    grad_decoded = back_mul(high_low, weights[21]) + back_mul(lowband_low, weights[23])
    grad_dec_in, dec_grads = block_backward(
        grad_decoded, weights[13:21], dec_kept, query_image, key_image, DHEADS
    )
    grad_token = jnp.sum(hidden[:, None] * grad_dec_in, axis=0)
    grad_projected = grad_dec_in * (1.0 - hidden)[:, None]
    projected_low = grad_projected.astype(jnp.bfloat16)
    grad_encoded = back_mul(projected_low, weights[10])
    grad_embedded, enc_grads = block_backward(
        grad_encoded, weights[2:10], enc_kept, query_image, key_image, HEADS
    )
    grads = (
        [outer(pixels, grad_embedded.astype(jnp.bfloat16)), jnp.sum(grad_embedded, axis=0)]
        + enc_grads
        + [outer(encoded_low, projected_low), jnp.sum(grad_projected, axis=0), grad_token]
        + dec_grads
        + [
            outer(decoded_low, high_low),
            jnp.sum(grad_high, axis=0),
            outer(decoded_low, lowband_low),
            jnp.sum(grad_low_pred, axis=0),
        ]
    )
    shard = master.shape[0]
    groups, seqs = (lax.axis_size("dp"), lax.axis_size("seq"))
    total_params = shard * groups * seqs
    used = sum((math.prod(shape) for shape in param_shapes()))
    grad_flat = jnp.concatenate(
        [g.reshape(-1) for g in grads] + [jnp.zeros((total_params - used,), jnp.float32)]
    )
    partial_share = lax.psum_scatter(
        grad_flat.reshape(groups, seqs, shard), "seq", scatter_dimension=1, tiled=True
    )
    summed = lax.psum(partial_share, "dp")
    owned = lax.dynamic_index_in_dim(summed, lax.axis_index("dp"), 0, keepdims=False)[0]
    square_sum = jnp.sum(owned * owned)
    loss_total, square_total = lax.psum((loss_local, square_sum), ("dp", "seq"))
    grad_norm = jnp.sqrt(square_total) / count
    clipped = owned * (jnp.minimum(1.0, clip_level / grad_norm) / count)
    first = 0.5 * moment_one + 0.5 * clipped
    second = 0.5 * moment_two + 0.5 * clipped * clipped
    step_value = step[0].astype(jnp.float32)
    correction = 1.0 - jnp.power(0.5, step_value)
    rate = peak_rate * jnp.minimum(1.0, step_value / warm_steps)
    new_master = master - rate * (
        first / correction / (jnp.sqrt(second / correction) + adam_eps) + decay_rate * master
    )
    return (new_master, first, second, (loss_total / count).reshape(1), grad_norm.reshape(1))


def solution(mesh):
    in_specs = (
        P(("dp", "seq"), None),
        P(("dp", "seq")),
        P("dp", None),
        P("dp", None),
        P("dp", None),
        P(),
        P(("dp", "seq")),
        P(("dp", "seq")),
        P(("dp", "seq")),
    )
    out_specs = (P(("dp", "seq")), P(("dp", "seq")), P(("dp", "seq")), P(), P())
    return jax.shard_map(body, mesh=mesh, in_specs=in_specs, out_specs=out_specs, check_vma=False)
```

profile of v0, /device:TPU:0, one launch (start us, length us, event | category | flops | bytes accessed | tf_op | source)
XLA Modules:
  0.0 3449.5 jit_solution(14075039186222475328)
XLA Ops:
  9.0 13.2 reshape.656
  23.9 23.2 all-gather.1
  50.9 345.3 %all-gather.16.cloned.1.call-done = bf16[32,1,548480]{2,1,0:T(2,128)(2,1)} async-done(((bf16[1,1,548480]{2,1,0:T(2,128)(2,1)}), bf16[32,1,548480]{2,1,0:T(2,128)(2,1)}) %all-gather.16.cloned.1.call-update) | async-done | bytes 35102736 | tf_op jit(solution)/shard_map/all_gather | solution.py:266
  396.2 220.1 %reduce.1 = bf16[32,548480]{1,0:T(8,128)(2,1)} reduce(bf16[32,1,548480]{2,1,0:T(2,128)(2,1)} %all-gather.16.cloned.1.call-done, bf16[]{:T(256)} %constant.289), dimensions={1}, to_apply=%all-gather.reduce_sub_computation | reduce | bytes 70205440 | tf_op jit(solution)/shard_map/all_gather | solution.py:266
  616.3 80.2 %reshape.657 = bf16[17551360]{0:T(1024)(128)(2,1)} reshape(bf16[32,548480]{1,0:T(8,128)(2,1)} %reduce.1) | data formatting | bytes 70205440
  728.4 11.4 fusion.139
  749.2 13.5 reshape.615
  762.6 13.5 slice.224
  791.7 10.9 fusion.2
  835.2 12.1 fusion.146
  875.8 25.4 all-gather.12.cloned.1.call-done
  947.8 11.3 fusion.149
  971.9 12.5 fusion.67
  1011.2 96.6 %reduce-scatter.3.cloned.1.call-done = f32[128,1024]{0,1:T(8,128)} async-done(((f32[2048,1024]{0,1:T(8,128)}), f32[128,1024]{0,1:T(8,128)}) %reduce-scatter.3.cloned.1.call-update) | async-done | bytes 524304 | tf_op jit(solution)/shard_map/reduce_scatter | solution.py:155
  1111.2 10.9 fusion.151
  1221.5 119.8 %reduce-scatter.5.cloned.1.call-done = f32[128,2048]{0,1:T(8,128)} async-done(((f32[2048,2048]{0,1:T(8,128)}), f32[128,2048]{0,1:T(8,128)}) %reduce-scatter.5.cloned.1.call-update) | async-done | bytes 1048592 | tf_op jit(solution)/shard_map/reduce_scatter | solution.py:155
  1357.7 12.3 copy.76
  1377.7 545.7 %concatenate.29 = f32[17551360]{0:T(1024)} concatenate(f32[786432]{0:T(1024)} %bitcast.185, f32[1024]{0:T(1024)} %get-tuple-element.14, f32[4096]{0:T(1024)S(1)} %bitcast.210, f32[3145728]{0:T(1024)} %bitcast.173, f32[1048576]{0:T(1024)} %bitcast.182, f32[1024]{0:T(1024)} %get-tuple-element.13, f32[4194304]{0:T(1024)} %bitcast.169, f32[4096]{0:T(1024)} %get-tuple-element.129, ...), dimensions={0} | concatenate | bytes 140410880 | tf_op jit(solution)/shard_map/concatenate | solution.py:342
  1923.4 68.2 %reshape.653 = f32[2,16,548480]{2,1,0:T(8,128)} reshape(f32[17551360]{0:T(1024)} %concatenate.29) | data formatting | bytes 140410880 | tf_op jit(solution)/shard_map/reshape | solution.py:346
  1991.6 113.0 %copy.72 = f32[2,16,548480]{2,0,1:T(2,128)} copy(f32[2,16,548480]{2,1,0:T(8,128)} %reshape.653) | data formatting | bytes 140410880 | tf_op jit(solution)/shard_map/reshape | solution.py:346
  2105.8 1137.4 %all-reduce.7.cloned.1.call-done = f32[2,16,548480]{2,0,1:T(2,128)} async-done(((f32[2,16,548480]{2,0,1:T(2,128)}), f32[2,16,548480]{2,0,1:T(2,128)}) %all-reduce.7.cloned.1.call-update) | async-done | bytes 70205456
  3251.3 110.4 %all-reduce.5.cloned.1.call-done = f32[2,1,548480]{2,0,1:T(2,128)} async-done(((f32[2,1,548480]{2,0,1:T(2,128)}), f32[2,1,548480]{2,0,1:T(2,128)}) %all-reduce.5.cloned.1.call-update) | async-done | bytes 4387856 | tf_op jit(solution)/shard_map/psum | solution.py:348
  3368.5 39.9 %all-reduce.1 = (f32[]{:T(128)}, f32[]{:T(128)}, f32[]{:T(128)}) all-reduce(f32[]{:T(128)} %get-tuple-element.30, f32[]{:T(128)} %multiply_reduce_fusion.1, f32[]{:T(128)} %get-tuple-element.29), channel_id=1, replica_groups=mesh['dp'=2,'seq'=16] {'dp','seq'}, use_global_device_ids=true, to_apply=%region_52.53 | all-reduce | flops 3 | bytes 24 | tf_op jit(solution)/shard_map/psum | solution.py:276
  3412.5 24.0 multiply_reduce_fusion
  (405 shorter events, 355.8 us)
Async XLA Ops:
  7.2 389.1 %all-gather.16.cloned.1.call-start = ((), (), s32[]{:S(2)}) async-start(), calls=%async_computation.9 | async-start | bytes 72399360 | tf_op jit(solution)/shard_map/all_gather | solution.py:266
  22.3 762.8 %all-gather.8.cloned.1.call-start = ((), (), s32[]{:S(2)}) async-start(), calls=%async_computation.2 | async-start | bytes 4456448 | tf_op jit(solution)/shard_map/all_gather | solution.py:174
  23.3 23.9 copy-start.87
  712.4 134.9 %copy-start.5 = (f32[128,1024]{1,0:T(8,128)}, f32[128,1024]{1,0:T(8,128)S(1)}, u32[]{:S(2)}) copy-start(f32[128,1024]{1,0:T(8,128)S(1)} %get-tuple-element.109) | copy-start | bytes 1572868
  728.4 100.1 %all-gather.10.cloned.1.call-start = ((), (), s32[]{:S(2)}) async-start(), calls=%async_computation.3 | async-start | bytes 4456448 | tf_op jit(solution)/shard_map/all_gather | solution.py:175
  739.8 161.4 %all-gather.12.cloned.1.call-start = ((), (), s32[]{:S(2)}) async-start(), calls=%async_computation.4 | async-start | bytes 2228224 | tf_op jit(solution)/shard_map/all_gather | solution.py:174
  746.8 44.8 %copy-start.20 = (bf16[128,1024]{0,1:T(8,128)(2,1)}, bf16[128,1024]{0,1:T(8,128)(2,1)S(1)}, u32[]{:S(2)}) copy-start(bf16[128,1024]{0,1:T(8,128)(2,1)S(1)} %copy.63) | copy-start | bytes 786436
  861.1 82.3 %all-gather.14.cloned.1.call-start = ((), (), s32[]{:S(2)}) async-start(), calls=%async_computation.5 | async-start | bytes 2228224 | tf_op jit(solution)/shard_map/all_gather | solution.py:175
  863.3 244.5 %reduce-scatter.3.cloned.1.call-start = ((), (), s32[]{:S(2)}) async-start(), calls=%async_computation.6 | async-start | bytes 8912896 | tf_op jit(solution)/shard_map/reduce_scatter | solution.py:155
  875.8 29.3 copy-start.12
  1004.0 104.9 %copy-start.14 = (bf16[512,1536]{1,0:T(8,128)(2,1)S(1)}, bf16[512,1536]{1,0:T(8,128)(2,1)}, u32[]{:S(2)}) copy-start(bf16[512,1536]{1,0:T(8,128)(2,1)} %reshape.616) | copy-start | bytes 4718596
  1004.0 337.3 %reduce-scatter.5.cloned.1.call-start = ((), (), s32[]{:S(2)}) async-start(), calls=%async_computation.7 | async-start | bytes 17825792 | tf_op jit(solution)/shard_map/reduce_scatter | solution.py:155
  1011.1 98.8 %copy-start.47 = (bf16[16,32,128]{2,1,0:T(8,128)(2,1)}, bf16[16,32,128]{2,1,0:T(8,128)(2,1)S(1)}, u32[]{:S(2)}) copy-start(bf16[16,32,128]{2,1,0:T(8,128)(2,1)S(1)} %fusion.24) | copy-start | bytes 393220
  1011.2 98.8 %copy-start.82 = (f32[128]{0:T(128)S(1)}, f32[128]{0:T(128)}, u32[]{:S(2)}) copy-start(f32[128]{0:T(128)} %get-tuple-element.44) | copy-start | bytes 1540
  1162.9 2080.3 %all-reduce.7.cloned.1.call-start = ((), (), s32[]{:S(2)}) async-start(), calls=%async_computation.10 | async-start | bytes 140410880
  1218.5 124.1 %copy-start.6 = (f32[128,1024]{1,0:T(8,128)S(1)}, f32[128,1024]{1,0:T(8,128)}, u32[]{:S(2)}) copy-start(f32[128,1024]{1,0:T(8,128)} %copy-done.5) | copy-start | bytes 1572868
  1218.5 124.1 %copy-start.54 = (f32[1024]{0:T(1024)S(1)}, f32[1024]{0:T(1024)}, u32[]{:S(2)}) copy-start(f32[1024]{0:T(1024)} %copy-done.53) | copy-start | bytes 12292
  1218.5 124.1 %copy-start.56 = (f32[1024]{0:T(1024)S(1)}, f32[1024]{0:T(1024)}, u32[]{:S(2)}) copy-start(f32[1024]{0:T(1024)} %copy-done.55) | copy-start | bytes 12292
  1218.5 124.1 %copy-start.75 = (f32[128]{0:T(128)S(1)}, f32[128]{0:T(128)}, u32[]{:S(2)}) copy-start(f32[128]{0:T(128)} %copy-done.74) | copy-start | bytes 1540
  1218.6 124.1 %copy-start.77 = (f32[128]{0:T(128)S(1)}, f32[128]{0:T(128)}, u32[]{:S(2)}) copy-start(f32[128]{0:T(128)} %copy-done.76) | copy-start | bytes 1540
  2104.6 1257.1 %all-reduce.5.cloned.1.call-start = ((), (), s32[]{:S(2)}) async-start(), calls=%async_computation.8 | async-start | bytes 8775680 | tf_op jit(solution)/shard_map/psum | solution.py:348
  3249.8 186.7 %copy-start.25 = (f32[548480]{0:T(1024)S(1)}, f32[548480]{0:T(1024)}, u32[]{:S(2)}) copy-start(f32[548480]{0:T(1024)} %param.16) | copy-start | bytes 6581764
  3412.5 24.0 copy-start.9
  3412.5 24.0 copy-start.24
  (98 other events, 594.7 us)
Sparse Core Ops, SparseCore 0:
  22.4 373.7 all-gather.15
  728.5 48.7 all-gather.7
  779.4 49.0 all-gather.9
  861.3 39.8 all-gather.11
  903.2 40.1 all-gather.13
  1004.2 103.5 reduce-scatter.2
  1163.0 178.3 reduce-scatter.4
  2104.7 1138.4 all-reduce.6
  3249.9 111.6 all-reduce.4
where the time goes:
time: 3490 us; the launch traced here: 3450 us
  waiting for transfers between devices  1850 us (53%)
  local copies, waits for them, and re-layouts  1010 us (29%)
  other arithmetic  329 us (9%)
  matrix products  173 us (5%)
  blocking collectives  63.1 us (2%)
    unnamed x10, waiting for transfers between devices  1140 us
    concatenate x1, local copies, waits for them, and re-layouts, body(): jnp.concatenate([g.reshape(-1) for g in grads] + [jnp.zeros((total_params...  546 us
    all_gather x1, waiting for transfers between devices, body(): lax.all_gather(master.astype(jnp.bfloat16), ('dp', 'seq'), axis=0, tiled=...  345 us
    all_gather x1, other arithmetic, body(): lax.all_gather(master.astype(jnp.bfloat16), ('dp', 'seq'), axis=0, tiled=...  220 us
    reduce_scatter x2, waiting for transfers between devices, attend_back(): lax.psum_scatter(jnp.concatenate([grad_keys.reshape(count, -1), grad_valu...  216 us
    reshape x2, local copies, waits for them, and re-layouts, body(): grad_flat.reshape(groups, seqs, shard)  181 us
    unnamed x235, local copies, waits for them, and re-layouts  160 us
    psum x1, waiting for transfers between devices, body(): summed = lax.psum(partial_share, 'dp')  110 us
  transfers between devices with their start and end apart: 9, of which 8 were waited for; matrix products, arithmetic and copies ran while one was open for 6% of the time, Pallas kernels for 0%

commit v1 on v0

--- a/solution.py
+++ b/solution.py
@@ -345,7 +345,7 @@
     partial_share = lax.psum_scatter(
         grad_flat.reshape(groups, seqs, shard), "seq", scatter_dimension=1, tiled=True
     )
-    summed = lax.psum(partial_share, "dp")
+    summed = jnp.sum(lax.all_gather(partial_share, "dp"), axis=0)
     owned = lax.dynamic_index_in_dim(summed, lax.axis_index("dp"), 0, keepdims=False)[0]
     square_sum = jnp.sum(owned * owned)
     loss_total, square_total = lax.psum((loss_local, square_sum), ("dp", "seq"))

time: 3490 us -> 3640 us (1.043)
  other arithmetic: 329 us -> 449 us
    psum x1 -> x0, waiting for transfers between devices: 110 us -> none  [body(): summed = lax.psum(partial_share, 'dp')]
    all_gather x0 -> x1, waiting for transfers between devices: none -> 109 us  [body(): summed = jnp.sum(lax.all_gather(partial_share, 'dp'), axis=0)]
    all_gather x0 -> x1, other arithmetic: none -> 97 us  [body(): summed = jnp.sum(lax.all_gather(partial_share, 'dp'), axis=0)]
where the time goes in v1:
time: 3640 us; the launch traced here: 3590 us
  waiting for transfers between devices  1850 us (51%)
  local copies, waits for them, and re-layouts  1030 us (28%)
  other arithmetic  449 us (12%)
  matrix products  173 us (5%)
  blocking collectives  62.8 us (2%)
    unnamed x10, waiting for transfers between devices  1140 us
    concatenate x1, local copies, waits for them, and re-layouts, body(): jnp.concatenate([g.reshape(-1) for g in grads] + [jnp.zeros((total_params...  546 us
    all_gather x1, waiting for transfers between devices, body(): lax.all_gather(master.astype(jnp.bfloat16), ('dp', 'seq'), axis=0, tiled=...  345 us
    all_gather x1, other arithmetic, body(): lax.all_gather(master.astype(jnp.bfloat16), ('dp', 'seq'), axis=0, tiled=...  220 us
    reduce_scatter x2, waiting for transfers between devices, attend_back(): lax.psum_scatter(jnp.concatenate([grad_keys.reshape(count, -1), grad_valu...  217 us
    reshape x2, local copies, waits for them, and re-layouts, body(): grad_flat.reshape(groups, seqs, shard)  181 us
    unnamed x235, local copies, waits for them, and re-layouts  157 us
    all_gather x1, waiting for transfers between devices, body(): summed = jnp.sum(lax.all_gather(partial_share, 'dp'), axis=0)  109 us
  transfers between devices with their start and end apart: 9, of which 8 were waited for; matrix products, arithmetic and copies ran while one was open for 6% of the time, Pallas kernels for 0%

profile of v1, /device:TPU:0, one launch (start us, length us, event | category | flops | bytes accessed | tf_op | source)
XLA Modules:
  0.0 3592.4 jit_solution(932817037744513934)
XLA Ops:
  9.0 13.2 reshape.661
  23.9 23.2 all-gather.2
  51.0 345.3 %all-gather.20.cloned.1.call-done = bf16[32,1,548480]{2,1,0:T(2,128)(2,1)} async-done(((bf16[1,1,548480]{2,1,0:T(2,128)(2,1)}), bf16[32,1,548480]{2,1,0:T(2,128)(2,1)}) %all-gather.20.cloned.1.call-update) | async-done | bytes 35102736 | tf_op jit(solution)/shard_map/all_gather | solution.py:266
  396.2 220.1 %reduce.3 = bf16[32,548480]{1,0:T(8,128)(2,1)} reduce(bf16[32,1,548480]{2,1,0:T(2,128)(2,1)} %all-gather.20.cloned.1.call-done, bf16[]{:T(256)} %constant.289), dimensions={1}, to_apply=%all-gather.1.reduce_sub_computation | reduce | bytes 70205440 | tf_op jit(solution)/shard_map/all_gather | solution.py:266
  616.3 80.1 %reshape.662 = bf16[17551360]{0:T(1024)(128)(2,1)} reshape(bf16[32,548480]{1,0:T(8,128)(2,1)} %reduce.3) | data formatting | bytes 70205440
  728.2 11.4 fusion.139
  748.9 13.5 reshape.618
  762.4 13.5 slice.224
  835.0 12.1 fusion.146
  875.5 25.5 all-gather.14.cloned.1.call-done
  971.7 12.5 fusion.67
  1010.7 96.6 %reduce-scatter.3.cloned.1.call-done = f32[128,1024]{0,1:T(8,128)} async-done(((f32[2048,1024]{0,1:T(8,128)}), f32[128,1024]{0,1:T(8,128)}) %reduce-scatter.3.cloned.1.call-update) | async-done | bytes 524304 | tf_op jit(solution)/shard_map/reduce_scatter | solution.py:155
  1220.8 120.0 %reduce-scatter.5.cloned.1.call-done = f32[128,2048]{0,1:T(8,128)} async-done(((f32[2048,2048]{0,1:T(8,128)}), f32[128,2048]{0,1:T(8,128)}) %reduce-scatter.5.cloned.1.call-update) | async-done | bytes 1048592 | tf_op jit(solution)/shard_map/reduce_scatter | solution.py:155
  1357.1 12.2 copy.80
  1377.0 545.6 %concatenate.29 = f32[17551360]{0:T(1024)} concatenate(f32[786432]{0:T(1024)} %bitcast.185, f32[1024]{0:T(1024)} %get-tuple-element.14, f32[4096]{0:T(1024)S(1)} %bitcast.210, f32[3145728]{0:T(1024)} %bitcast.173, f32[1048576]{0:T(1024)} %bitcast.182, f32[1024]{0:T(1024)} %get-tuple-element.13, f32[4194304]{0:T(1024)} %bitcast.169, f32[4096]{0:T(1024)} %get-tuple-element.129, ...), dimensions={0} | concatenate | bytes 140410880 | tf_op jit(solution)/shard_map/concatenate | solution.py:342
  1922.7 67.9 %reshape.656 = f32[2,16,548480]{2,1,0:T(8,128)} reshape(f32[17551360]{0:T(1024)} %concatenate.29) | data formatting | bytes 140410880 | tf_op jit(solution)/shard_map/reshape | solution.py:346
  1990.6 113.0 %copy.74 = f32[2,16,548480]{2,0,1:T(2,128)} copy(f32[2,16,548480]{2,1,0:T(8,128)} %reshape.656) | data formatting | bytes 140410880 | tf_op jit(solution)/shard_map/reshape | solution.py:346
  2104.8 1137.3 %all-reduce.4.cloned.1.call-done = f32[2,16,548480]{2,0,1:T(2,128)} async-done(((f32[2,16,548480]{2,0,1:T(2,128)}), f32[2,16,548480]{2,0,1:T(2,128)}) %all-reduce.4.cloned.1.call-update) | async-done | bytes 70205456
  3255.4 109.2 %all-gather.18.cloned.1.call-done = f32[4,1,548480]{2,1,0:T(1,128)} async-done(((f32[2,1,548480]{2,1,0:T(1,128)}), f32[4,1,548480]{2,1,0:T(1,128)}) %all-gather.18.cloned.1.call-update) | async-done | bytes 8775696 | tf_op jit(solution)/shard_map/all_gather | solution.py:348
  3364.6 97.0 %reduce.4 = f32[4,548480]{1,0:T(4,128)} reduce(f32[4,1,548480]{2,1,0:T(1,128)} %all-gather.18.cloned.1.call-done, f32[]{:T(128)} %constant.290), dimensions={1}, to_apply=%all-gather.reduce_sub_computation | reduce | bytes 17551364 | tf_op jit(solution)/shard_map/all_gather | solution.py:348
  3461.6 20.1 reshape.659
  3481.7 23.2 reduce.2
  3511.7 39.6 %all-reduce.1 = (f32[]{:T(128)}, f32[]{:T(128)}, f32[]{:T(128)}) all-reduce(f32[]{:T(128)} %get-tuple-element.30, f32[]{:T(128)} %multiply_reduce_fusion.1, f32[]{:T(128)} %get-tuple-element.29), channel_id=1, replica_groups=mesh['dp'=2,'seq'=16] {'dp','seq'}, use_global_device_ids=true, to_apply=%region_52.53 | all-reduce | flops 3 | bytes 24 | tf_op jit(solution)/shard_map/psum | solution.py:276
  3555.5 24.0 multiply_reduce_fusion
  (409 shorter events, 393.6 us)
Async XLA Ops:
  7.2 389.1 %all-gather.20.cloned.1.call-start = ((), (), s32[]{:S(2)}) async-start(), calls=%async_computation.9 | async-start | bytes 72399360 | tf_op jit(solution)/shard_map/all_gather | solution.py:266
  22.3 762.6 %all-gather.10.cloned.1.call-start = ((), (), s32[]{:S(2)}) async-start(), calls=%async_computation.2 | async-start | bytes 4456448 | tf_op jit(solution)/shard_map/all_gather | solution.py:174
  23.3 23.9 copy-start.87
  712.2 135.0 %copy-start.5 = (f32[128,1024]{1,0:T(8,128)}, f32[128,1024]{1,0:T(8,128)S(1)}, u32[]{:S(2)}) copy-start(f32[128,1024]{1,0:T(8,128)S(1)} %get-tuple-element.109) | copy-start | bytes 1572868
  728.2 100.1 %all-gather.12.cloned.1.call-start = ((), (), s32[]{:S(2)}) async-start(), calls=%async_computation.3 | async-start | bytes 4456448 | tf_op jit(solution)/shard_map/all_gather | solution.py:175
  739.6 161.3 %all-gather.14.cloned.1.call-start = ((), (), s32[]{:S(2)}) async-start(), calls=%async_computation.4 | async-start | bytes 2228224 | tf_op jit(solution)/shard_map/all_gather | solution.py:174
  746.6 44.7 %copy-start.20 = (bf16[128,1024]{0,1:T(8,128)(2,1)}, bf16[128,1024]{0,1:T(8,128)(2,1)S(1)}, u32[]{:S(2)}) copy-start(bf16[128,1024]{0,1:T(8,128)(2,1)S(1)} %copy.65) | copy-start | bytes 786436
  860.9 82.3 %all-gather.16.cloned.1.call-start = ((), (), s32[]{:S(2)}) async-start(), calls=%async_computation.5 | async-start | bytes 2228224 | tf_op jit(solution)/shard_map/all_gather | solution.py:175
  863.0 244.3 %reduce-scatter.3.cloned.1.call-start = ((), (), s32[]{:S(2)}) async-start(), calls=%async_computation.6 | async-start | bytes 8912896 | tf_op jit(solution)/shard_map/reduce_scatter | solution.py:155
  875.5 29.4 copy-start.12
  1003.6 104.9 %copy-start.14 = (bf16[512,1536]{1,0:T(8,128)(2,1)S(1)}, bf16[512,1536]{1,0:T(8,128)(2,1)}, u32[]{:S(2)}) copy-start(bf16[512,1536]{1,0:T(8,128)(2,1)} %reshape.619) | copy-start | bytes 4718596
  1003.6 337.3 %reduce-scatter.5.cloned.1.call-start = ((), (), s32[]{:S(2)}) async-start(), calls=%async_computation.7 | async-start | bytes 17825792 | tf_op jit(solution)/shard_map/reduce_scatter | solution.py:155
  1010.7 98.8 %copy-start.47 = (bf16[16,32,128]{2,1,0:T(8,128)(2,1)}, bf16[16,32,128]{2,1,0:T(8,128)(2,1)S(1)}, u32[]{:S(2)}) copy-start(bf16[16,32,128]{2,1,0:T(8,128)(2,1)S(1)} %fusion.24) | copy-start | bytes 393220
  1010.7 98.8 %copy-start.82 = (f32[128]{0:T(128)S(1)}, f32[128]{0:T(128)}, u32[]{:S(2)}) copy-start(f32[128]{0:T(128)} %get-tuple-element.44) | copy-start | bytes 1540
  1162.4 2079.8 %all-reduce.4.cloned.1.call-start = ((), (), s32[]{:S(2)}) async-start(), calls=%async_computation.10 | async-start | bytes 140410880
  1217.8 124.3 %copy-start.6 = (f32[128,1024]{1,0:T(8,128)S(1)}, f32[128,1024]{1,0:T(8,128)}, u32[]{:S(2)}) copy-start(f32[128,1024]{1,0:T(8,128)} %copy-done.5) | copy-start | bytes 1572868
  1217.8 124.3 %copy-start.54 = (f32[1024]{0:T(1024)S(1)}, f32[1024]{0:T(1024)}, u32[]{:S(2)}) copy-start(f32[1024]{0:T(1024)} %copy-done.53) | copy-start | bytes 12292
  1217.8 124.3 %copy-start.56 = (f32[1024]{0:T(1024)S(1)}, f32[1024]{0:T(1024)}, u32[]{:S(2)}) copy-start(f32[1024]{0:T(1024)} %copy-done.55) | copy-start | bytes 12292
  1217.8 124.3 %copy-start.75 = (f32[128]{0:T(128)S(1)}, f32[128]{0:T(128)}, u32[]{:S(2)}) copy-start(f32[128]{0:T(128)} %copy-done.74) | copy-start | bytes 1540
  1217.8 124.3 %copy-start.77 = (f32[128]{0:T(128)S(1)}, f32[128]{0:T(128)}, u32[]{:S(2)}) copy-start(f32[128]{0:T(128)} %copy-done.76) | copy-start | bytes 1540
  2103.6 1261.0 %all-gather.18.cloned.1.call-start = ((), (), s32[]{:S(2)}) async-start(), calls=%async_computation.8 | async-start | bytes 13163520 | tf_op jit(solution)/shard_map/all_gather | solution.py:348
  3481.7 97.7 %copy-start.25 = (f32[548480]{0:T(1024)S(1)}, f32[548480]{0:T(1024)}, u32[]{:S(2)}) copy-start(f32[548480]{0:T(1024)} %param.16) | copy-start | bytes 6581764
  3555.4 24.0 copy-start.9
  3555.4 24.0 copy-start.24
  (98 other events, 593.4 us)
Sparse Core Ops, SparseCore 0:
  22.4 373.7 all-gather.19
  728.3 48.7 all-gather.9
  779.2 49.0 all-gather.11
  861.0 39.8 all-gather.13
  902.9 40.1 all-gather.15
  1003.7 103.5 reduce-scatter.2
  1162.5 178.2 reduce-scatter.4
  2103.8 1138.3 all-reduce.3
  3254.2 110.3 all-gather.17
